TPU v7x, 32 devices: a whole 2x2x4 slice. The times are simulated.
32 devices in a mesh: tm: 8 (over z, core), zone: 4 (over y, x).
Axes of the slice: x: 2, y: 2, z: 4, core: 2. Of those that a mesh axis runs over, the one named last changes fastest.
Arguments:
- initial_guess: float32 [15, 3, 4, 1024], P(None, None, 'zone', 'tm'), may hold values from -2.5 to 2.5
- harmonic_loads: float32 [15, 3, 4, 1024], P(None, None, 'zone', 'tm'), may hold values from -12 to 12
- stiffness: bfloat16 [4, 8, 5, 384, 384], P('zone', 'tm'), as said below
- mass_tiles: bfloat16 [4, 8, 384, 384], P('zone', 'tm'), as said below
- block_links: int32 [4, 8, 2], P('zone', 'tm'), may hold values from 0 to 7, as said below
- states: int32 [2048, 4, 1024], P('tm', 'zone'), may hold values from 0 to 2
- preload: float32 [4, 1024], P('zone'), may hold values from 1 to 3
- normal_stiff: float32 [4, 1024], P('zone'), may hold values from 0.5 to 2
- tangent_stiff: float32 [4, 1024], P('zone'), may hold values from 0.3 to 1.5
- friction: float32 [4, 1024], P('zone'), may hold values from 0.2 to 0.8
Outputs:
- coefficients: float32 [15, 3, 4, 1024], P(None, None, 'zone', 'tm')
- residual: float32 [15, 3, 4, 1024], P(None, None, 'zone', 'tm')
Inputs may be any that keep to these rules, and one draw needn't show every extreme that they name: `block_links`: in each row the 2 entries are distinct and differ from the row's own block index (the second index). `stiffness`: in slot 0 every diagonal entry lies between 4 and 8. `mass_tiles`: every diagonal entry lies between 0.5 and 1.
All inputs are finite; a program needn't handle non-finite values.
Results may differ from a plain program's by a relative error of at most 0.0003.
Values sent between devices are 32-bit elements; how exact they have to be, the bound alone decides.
A program may use at most 64 MiB of HBM per device.

v0:
```python
import math
import jax
import jax.numpy as jnp
from jax import lax
from jax.sharding import PartitionSpec as P

DIRS = 3
BLOCK = 128
ITERS = 2
OMEGA_SQUARED = 0.05
SMOOTHING = 0.1
FULL_PRECISION = lax.Precision.HIGHEST


def padded(cells, sides, width):
    for axis, dim in sides:
        count = lax.axis_size(axis)
        head = lax.slice_in_dim(cells, 0, width, axis=dim)
        tail = lax.slice_in_dim(cells, cells.shape[dim] - width, cells.shape[dim], axis=dim)
        cells = jnp.concatenate(
            [
                lax.ppermute(tail, axis, [(i, (i + 1) % count) for i in range(count)]),
                cells,
                lax.ppermute(head, axis, [((i + 1) % count, i) for i in range(count)]),
            ],
            axis=dim,
        )
    return cells


def harmonic_orders(coeff_count):
    row_index = jnp.arange(coeff_count, dtype=jnp.int32)
    return (row_index + 1) // 2


def synthesis_table(first_sample, sample_count, total_samples, coeff_count):
    samples_here = first_sample + jnp.arange(sample_count, dtype=jnp.int32)
    orders = harmonic_orders(coeff_count)
    phases = samples_here[:, None] * orders[None, :] % total_samples
    angles = phases.astype(jnp.float32) * (2.0 * math.pi / total_samples)
    row_index = jnp.arange(coeff_count, dtype=jnp.int32)
    is_sine = (row_index % 2 == 0) & (row_index > 0)
    return jnp.where(is_sine[None, :], jnp.sin(angles), jnp.cos(angles))


def analysis_table(synthesis, coeff_count, total_samples):
    orders = harmonic_orders(coeff_count)
    scaling = jnp.where(orders == 0, 1.0, 2.0) / total_samples
    return synthesis * scaling[None, :]


def contact_law(motion, states, preload, normal_stiff, tangent_stiff, friction):
    normal_part = preload + normal_stiff * motion[:, 0]
    slide_one = motion[:, 1]
    slide_two = motion[:, 2]
    magnitude = jnp.sqrt(slide_one * slide_one + slide_two * slide_two + SMOOTHING * SMOOTHING)
    touching = states > 0
    sticking = states == 1
    normal_force = jnp.where(touching, normal_part, 0.0)
    slip_factor = friction * normal_force / magnitude
    tangent_factor = jnp.where(sticking, tangent_stiff, slip_factor)
    tangent_factor = jnp.where(touching, tangent_factor, 0.0)
    return jnp.stack([normal_force, tangent_factor * slide_one, tangent_factor * slide_two], axis=1)


def block_view(coeff_field):
    coeff_count, direction_count, node_count = coeff_field.shape
    divided = coeff_field.reshape(coeff_count, direction_count, node_count // BLOCK, BLOCK)
    return divided.transpose(2, 0, 1, 3).reshape(
        node_count // BLOCK, coeff_count, direction_count * BLOCK
    )


def field_view(blocks):
    block_count, coeff_count, block_width = blocks.shape
    divided = blocks.reshape(block_count, coeff_count, DIRS, BLOCK)
    return divided.transpose(1, 2, 0, 3).reshape(coeff_count, DIRS, block_count * BLOCK)


def coupled_update(
    own_field, zone_coeffs, sectors, stiffness, mass_tiles, block_links, forces, own_loads
):
    orders = harmonic_orders(own_field.shape[0]).astype(jnp.float32)
    inertia = OMEGA_SQUARED * orders * orders
    own_blocks = block_view(own_field)
    zone_blocks = block_view(zone_coeffs)
    before_blocks = block_view(sectors[:, :, 0, :])
    after_blocks = block_view(sectors[:, :, 2, :])
    linked = zone_blocks[block_links]
    sources = jnp.concatenate(
        [own_blocks[:, None], before_blocks[:, None], after_blocks[:, None], linked], axis=1
    )
    elastic = jnp.einsum(
        "bshi,bsij->bhj", sources, stiffness.astype(jnp.float32), precision=FULL_PRECISION
    )
    kinetic = jnp.einsum(
        "bhi,bij->bhj", own_blocks, mass_tiles.astype(jnp.float32), precision=FULL_PRECISION
    )
    coupled = elastic - inertia[None, :, None] * kinetic
    residual = field_view(coupled) + forces - own_loads
    stiff_diag = jnp.diagonal(stiffness[:, 0].astype(jnp.float32), axis1=-2, axis2=-1)
    mass_diag = jnp.diagonal(mass_tiles.astype(jnp.float32), axis1=-2, axis2=-1)
    pivots = stiff_diag[:, None, :] - inertia[None, :, None] * mass_diag[:, None, :]
    return (residual, own_field - residual / field_view(pivots))


def per_device(
    initial_guess,
    harmonic_loads,
    stiffness,
    mass_tiles,
    block_links,
    states,
    preload,
    normal_stiff,
    tangent_stiff,
    friction,
):
    coeff_count = initial_guess.shape[0]
    samples_dev = states.shape[0]
    total_samples = samples_dev * lax.axis_size("tm")
    own_field = initial_guess[:, :, 0, :]
    own_loads = harmonic_loads[:, :, 0, :]
    zone_states = states[:, 0, :]
    zone_preload = preload[0]
    zone_normal = normal_stiff[0]
    zone_tangent = tangent_stiff[0]
    zone_friction = friction[0]
    local_stiffness = stiffness[0]
    local_mass = mass_tiles[0]
    local_links = block_links[0]
    synthesis = synthesis_table(
        lax.axis_index("tm") * samples_dev, samples_dev, total_samples, coeff_count
    )
    analysis = analysis_table(synthesis, coeff_count, total_samples)
    residual = own_field
    for iteration in range(ITERS):
        zone_coeffs = lax.all_gather(own_field, "tm", axis=2, tiled=True)
        sectors = padded(own_field[:, :, None, :], (("zone", 2),), 1)
        motion = jnp.einsum("th,hdn->tdn", synthesis, zone_coeffs, precision=FULL_PRECISION)
        forces_time = contact_law(
            motion, zone_states, zone_preload, zone_normal, zone_tangent, zone_friction
        )
        partial_terms = jnp.einsum("th,tdn->hdn", analysis, forces_time, precision=FULL_PRECISION)
        forces = lax.psum_scatter(partial_terms, "tm", scatter_dimension=2, tiled=True)
        residual, own_field = coupled_update(
            own_field,
            zone_coeffs,
            sectors,
            local_stiffness,
            local_mass,
            local_links,
            forces,
            own_loads,
        )
    return (own_field[:, :, None, :], residual[:, :, None, :])


def solution(mesh):
    return jax.shard_map(
        per_device,
        mesh=mesh,
        in_specs=(
            P(None, None, "zone", "tm"),
            P(None, None, "zone", "tm"),
            P("zone", "tm", None, None, None),
            P("zone", "tm", None, None),
            P("zone", "tm", None),
            P("tm", "zone", None),
            P("zone", None),
            P("zone", None),
            P("zone", None),
            P("zone", None),
        ),
        out_specs=(P(None, None, "zone", "tm"), P(None, None, "zone", "tm")),
        check_vma=False,
    )
```

profile of v0, /device:TPU:0, one launch (start us, length us, event | category | flops | bytes accessed | tf_op | source)
XLA Modules:
  0.0 127.1 jit_solution(10812076237233174816)
XLA Ops:
  7.3 3.0 %collective-permute-start = (f32[15,3,1,128]{3,2,1,0:T(1,128)}, f32[15,3,1,128]{3,2,1,0:T(1,128)}, u32[]{:S(2)}, u32[]{:S(2)}) collective-permute-start(f32[15,3,1,128]{3,2,1,0:T(1,128)} %param.10), channel_id=1, source_target_pairs={{0,1},{1,2},{2,3},{3,0},{4,5},{5,6},{6,7},{7,4},{8,9},{9,10},{10,1... | collective-permute-start | bytes 69128 | tf_op jit(solution)/shard_map/ppermute | solution.py:22
  10.3 1.0 collective-permute-start.1
  11.3 0.8 copy.41
  12.1 14.8 %all-gather = f32[15,3,1,1024]{3,0,1,2:T(8,128)S(1)} all-gather(f32[15,3,1,128]{3,0,1,2:T(8,128)S(1)} %copy.41), channel_id=2, replica_groups=mesh['tm'=8,'zone'=4] {'tm'}, dimensions={3}, use_global_device_ids=true | all-gather | bytes 207360 | tf_op jit(solution)/shard_map/all_gather | solution.py:138
  26.9 2.8 %fusion.35 = f32[256,3,1024]{2,0,1:T(8,128)S(1)} fusion(f32[15,3,1,1024]{3,0,1,2:T(8,128)S(1)} %all-gather, s32[15]{0:T(128)S(1)} %and_select_fusion.1, s32[256]{0:T(256)S(1)} %iota_add_fusion, pred[15]{0:T(512)(128)(4,1)S(1)} %compare_and_fusion), kind=kOutput, calls=%fused_computation.45 | convolution fusion | flops 141615360 | bytes 3331147 | tf_op jit(solution)/shard_map/th,hdn->tdn/dot_general | solution.py:140
  29.7 0.8 fusion.31
  31.2 2.4 %fusion = f32[15,3,1024]{2,0,1:T(8,128)} fusion(f32[256,1,1024]{2,0,1:T(8,128)S(1)} %fusion.30, f32[256,1,1024]{2,0,1:T(8,128)S(1)} %get-tuple-element.12, f32[256,1,1024]{2,0,1:T(8,128)S(1)} %get-tuple-element.13, f32[15]{0:T(128)S(1)} %fusion.63, s32[15]{0:T(128)S(1)} %and_select_fusion.1, s32[256]{0:T(256)S(1)} %iota_add_fusion, ...), kind=kOutput, calls=%fused_computation.4 | convolution fusion | flops 143192064 | bytes 3331207 | tf_op jit(solution)/shard_map/th,tdn->hdn/dot_general | solution.py:144
  34.3 0.7 copy_bitcast_fusion.1
  35.7 1.6 %copy.44 = f32[8,15,384]{2,1,0:T(8,128)} copy(f32[8,15,384]{2,0,1:T(8,128)} %copy_bitcast_fusion.1) | data formatting | bytes 368640 | tf_op jit(solution)/shard_map/reshape | solution.py:69
  37.4 4.6 %gather_fusion.1 = f32[384]{0:T(512)} fusion(f32[384,384]{1,0:T(8,128)S(1)} %fusion.32, s32[384]{0:T(512)S(1)} %or_reduce_fusion), kind=kCustom, calls=%fused_computation.1 | custom fusion | bytes 6144 | tf_op jit(solution)/shard_map/jit(diagonal)/gather | solution.py:101
  42.0 3.4 %gather_fusion.2 = f32[384]{0:T(512)S(1)} fusion(f32[384,384]{1,0:T(8,128)S(1)} %bitcast_convert_fusion, s32[384]{0:T(512)S(1)} %or_reduce_fusion), kind=kCustom, calls=%fused_computation.2 | custom fusion | bytes 6144 | tf_op jit(solution)/shard_map/jit(diagonal)/gather | solution.py:102
  45.5 1.6 %gather_fusion = f32[2,15,384]{2,1,0:T(8,128)S(1)} fusion(f32[8,15,384]{2,1,0:T(8,128)} %copy.44, s32[1024]{0:T(1024)} %pad_clamp_fusion), kind=kCustom, calls=%fused_computation | custom fusion | bytes 92168 | tf_op jit(solution)/shard_map/gather | solution.py:89
  47.1 0.7 copy.46
  47.9 0.7 copy.47
  48.6 0.7 fusion.16
  49.6 14.5 %reduce-scatter.3.cloned.1.call-done = f32[15,3,128]{2,0,1:T(8,128)} async-done(((f32[15,3,1024]{2,0,1:T(8,128)}), f32[15,3,128]{2,0,1:T(8,128)}) %reduce-scatter.3.cloned.1.call-update) | async-done | bytes 23056 | tf_op jit(solution)/shard_map/reduce_scatter | solution.py:145
  64.1 0.8 fusion.50
  64.9 2.4 %collective-permute-start.3 = (f32[15,3,1,128]{3,0,1,2:T(8,128)S(1)}, f32[15,3,1,128]{3,0,1,2:T(8,128)S(1)}, u32[]{:S(2)}, u32[]{:S(2)}) collective-permute-start(f32[15,3,1,128]{3,0,1,2:T(8,128)S(1)} %bitcast.104), channel_id=1, source_target_pairs={{1,0},{2,1},{3,2},{0,3},{5,4},{6,5},{7,6},{4,7},{9,8},{10,9},{11,1... | collective-permute-start | bytes 69128 | tf_op jit(solution)/shard_map/ppermute | solution.py:24
  67.3 14.3 %all_gather.7 = f32[15,3,1024]{2,0,1:T(8,128)S(1)} all-gather(f32[15,3,128]{2,0,1:T(8,128)S(1)} %fusion.50), channel_id=1, replica_groups=mesh['tm'=8,'zone'=4] {'tm'}, dimensions={2}, use_global_device_ids=true | all-gather | bytes 207360 | tf_op jit(solution)/shard_map/all_gather | solution.py:138
  81.6 2.8 %fusion.54 = f32[256,3,1024]{2,0,1:T(8,128)S(1)} fusion(f32[15,3,1024]{2,0,1:T(8,128)S(1)} %all_gather.7, s32[15]{0:T(128)S(1)} %copy-done.18, s32[256]{0:T(256)S(1)} %copy-done.16, pred[15]{0:T(512)(128)(4,1)S(1)} %copy-done.20), kind=kOutput, calls=%fused_computation.79 | convolution fusion | flops 141615360 | bytes 3331147 | tf_op jit(solution)/shard_map/th,hdn->tdn/dot_general | solution.py:140
  85.8 2.4 %fusion.6 = f32[15,3,1024]{2,0,1:T(8,128)} fusion(f32[256,1,1024]{2,0,1:T(8,128)S(1)} %fusion.28, f32[256,1,1024]{2,0,1:T(8,128)S(1)} %get-tuple-element.10, f32[256,1,1024]{2,0,1:T(8,128)S(1)} %get-tuple-element.11, f32[15]{0:T(128)S(1)} %copy-done.23, s32[15]{0:T(128)S(1)} %copy-done.18, s32[256]{0:T(256)S(1)} %copy-done.16, pred[15]{0:T(512)(128)(4,1)S(1)} %copy-done.20), kind=kOutput, calls=%fused_computation.10 | convolution fusion | flops 143192064 | bytes 3331207 | tf_op jit(solution)/shard_map/th,tdn->hdn/dot_general | solution.py:144
  89.1 0.7 fusion.19
  90.1 28.1 %reduce-scatter.5.cloned.1.call-done = f32[15,3,128]{2,0,1:T(8,128)} async-done(((f32[15,3,1024]{2,0,1:T(8,128)}), f32[15,3,128]{2,0,1:T(8,128)}) %reduce-scatter.5.cloned.1.call-update) | async-done | bytes 23056 | tf_op jit(solution)/shard_map/reduce_scatter | solution.py:145
  118.2 0.8 subtract_bitcast_fusion
  (93 shorter events, 6.1 us)
Async XLA Ops:
  7.2 22.5 %copy-start.5 = (f32[1,1024]{1,0:T(1,128)S(1)}, f32[1,1024]{1,0:T(1,128)}, u32[]{:S(2)}) copy-start(f32[1,1024]{1,0:T(1,128)} %param.19) | copy-start | bytes 12292
  7.2 22.5 %copy-start.7 = (f32[1,1024]{1,0:T(1,128)S(1)}, f32[1,1024]{1,0:T(1,128)}, u32[]{:S(2)}) copy-start(f32[1,1024]{1,0:T(1,128)} %param.18) | copy-start | bytes 12292
  7.2 22.5 %copy-start.10 = (f32[1,1024]{1,0:T(1,128)S(1)}, f32[1,1024]{1,0:T(1,128)}, u32[]{:S(2)}) copy-start(f32[1,1024]{1,0:T(1,128)} %param.17) | copy-start | bytes 12292
  7.2 22.5 %copy-start.12 = (f32[1,1024]{1,0:T(1,128)S(1)}, f32[1,1024]{1,0:T(1,128)}, u32[]{:S(2)}) copy-start(f32[1,1024]{1,0:T(1,128)} %param.16) | copy-start | bytes 12292
  7.2 22.5 %copy-start.2 = (s32[256,1,1024]{2,1,0:T(1,128)S(1)}, s32[256,1,1024]{2,1,0:T(1,128)}, u32[]{:S(2)}) copy-start(s32[256,1,1024]{2,1,0:T(1,128)} %param.15) | copy-start | bytes 3145732
  7.2 56.8 %reduce-scatter.3.cloned.1.call-start = ((), (), s32[]{:S(2)}) async-start(), calls=%async_computation.2 | async-start | bytes 221184 | tf_op jit(solution)/shard_map/reduce_scatter | solution.py:145
  7.3 39.9 %collective-permute-start = (f32[15,3,1,128]{3,2,1,0:T(1,128)}, f32[15,3,1,128]{3,2,1,0:T(1,128)}, u32[]{:S(2)}, u32[]{:S(2)}) collective-permute-start(f32[15,3,1,128]{3,2,1,0:T(1,128)} %param.10), channel_id=1, source_target_pairs={{0,1},{1,2},{2,3},{3,0},{4,5},{5,6},{6,7},{7,4},{8,9},{9,10},{10,1... | collective-permute-start | bytes 69128 | tf_op jit(solution)/shard_map/ppermute | solution.py:22
  10.3 37.6 %collective-permute-start.1 = (f32[15,3,1,128]{3,2,1,0:T(1,128)}, f32[15,3,1,128]{3,2,1,0:T(1,128)}, u32[]{:S(2)}, u32[]{:S(2)}) collective-permute-start(f32[15,3,1,128]{3,2,1,0:T(1,128)} %param.10), channel_id=1, source_target_pairs={{1,0},{2,1},{3,2},{0,3},{5,4},{6,5},{7,6},{4,7},{9,8},{10,9},{11,1... | collective-permute-start | bytes 69128 | tf_op jit(solution)/shard_map/ppermute | solution.py:24
  11.3 19.8 %copy-start.17 = (s32[15]{0:T(128)}, s32[15]{0:T(128)S(1)}, u32[]{:S(2)}) copy-start(s32[15]{0:T(128)S(1)} %and_select_fusion.1) | copy-start | bytes 184
  11.3 19.8 %copy-start.19 = (pred[15]{0:T(512)(128)(4,1)}, pred[15]{0:T(512)(128)(4,1)S(1)}, u32[]{:S(2)}) copy-start(pred[15]{0:T(512)(128)(4,1)S(1)} %compare_and_fusion) | copy-start | bytes 49
  11.3 19.8 %copy-start.22 = (f32[15]{0:T(128)}, f32[15]{0:T(128)S(1)}, u32[]{:S(2)}) copy-start(f32[15]{0:T(128)S(1)} %fusion.63) | copy-start | bytes 184
  12.1 19.1 %copy-start.15 = (s32[256]{0:T(256)}, s32[256]{0:T(256)S(1)}, u32[]{:S(2)}) copy-start(s32[256]{0:T(256)S(1)} %iota_add_fusion) | copy-start | bytes 3076
  33.6 84.7 %reduce-scatter.5.cloned.1.call-start = ((), (), s32[]{:S(2)}) async-start(), calls=%async_computation.3 | async-start | bytes 221184 | tf_op jit(solution)/shard_map/reduce_scatter | solution.py:145
  42.0 22.1 %copy-start.4 = (f32[15,3,1,128]{3,2,1,0:T(1,128)S(1)}, f32[15,3,1,128]{3,2,1,0:T(1,128)}, u32[]{:S(2)}) copy-start(f32[15,3,1,128]{3,2,1,0:T(1,128)} %param.11) | copy-start | bytes 69124
  42.0 22.1 %copy-start.9 = (f32[384]{0:T(512)S(1)}, f32[384]{0:T(512)}, u32[]{:S(2)}) copy-start(f32[384]{0:T(512)} %gather_fusion.1) | copy-start | bytes 4612
  42.0 39.7 %copy-start.16 = (s32[256]{0:T(256)S(1)}, s32[256]{0:T(256)}, u32[]{:S(2)}) copy-start(s32[256]{0:T(256)} %copy-done.15) | copy-start | bytes 3076
  42.0 39.7 %copy-start.18 = (s32[15]{0:T(128)S(1)}, s32[15]{0:T(128)}, u32[]{:S(2)}) copy-start(s32[15]{0:T(128)} %copy-done.17) | copy-start | bytes 184
  42.0 39.7 %copy-start.20 = (pred[15]{0:T(512)(128)(4,1)S(1)}, pred[15]{0:T(512)(128)(4,1)}, u32[]{:S(2)}) copy-start(pred[15]{0:T(512)(128)(4,1)} %copy-done.19) | copy-start | bytes 49
  45.4 39.0 %copy-start.6 = (f32[1,1024]{1,0:T(1,128)S(1)}, f32[1,1024]{1,0:T(1,128)}, u32[]{:S(2)}) copy-start(f32[1,1024]{1,0:T(1,128)} %param.19) | copy-start | bytes 12292
  45.5 39.0 %copy-start.8 = (f32[1,1024]{1,0:T(1,128)S(1)}, f32[1,1024]{1,0:T(1,128)}, u32[]{:S(2)}) copy-start(f32[1,1024]{1,0:T(1,128)} %param.18) | copy-start | bytes 12292
  45.5 39.0 %copy-start.11 = (f32[1,1024]{1,0:T(1,128)S(1)}, f32[1,1024]{1,0:T(1,128)}, u32[]{:S(2)}) copy-start(f32[1,1024]{1,0:T(1,128)} %param.17) | copy-start | bytes 12292
  45.5 39.0 %copy-start.13 = (f32[1,1024]{1,0:T(1,128)S(1)}, f32[1,1024]{1,0:T(1,128)}, u32[]{:S(2)}) copy-start(f32[1,1024]{1,0:T(1,128)} %param.16) | copy-start | bytes 12292
  64.9 24.1 %collective-permute-start.3 = (f32[15,3,1,128]{3,0,1,2:T(8,128)S(1)}, f32[15,3,1,128]{3,0,1,2:T(8,128)S(1)}, u32[]{:S(2)}, u32[]{:S(2)}) collective-permute-start(f32[15,3,1,128]{3,0,1,2:T(8,128)S(1)} %bitcast.104), channel_id=1, source_target_pairs={{1,0},{2,1},{3,2},{0,3},{5,4},{6,5},{7,6},{4,7},{9,8},{10,9},{11,1... | collective-permute-start | bytes 69128 | tf_op jit(solution)/shard_map/ppermute | solution.py:24
  67.3 21.7 %collective-permute-start.2 = (f32[15,3,1,128]{3,0,1,2:T(8,128)S(1)}, f32[15,3,1,128]{3,0,1,2:T(8,128)S(1)}, u32[]{:S(2)}, u32[]{:S(2)}) collective-permute-start(f32[15,3,1,128]{3,0,1,2:T(8,128)S(1)} %bitcast.105), channel_id=1, source_target_pairs={{0,1},{1,2},{2,3},{3,0},{4,5},{5,6},{6,7},{7,4},{8,9},{9,10},{10,1... | collective-permute-start | bytes 69128 | tf_op jit(solution)/shard_map/ppermute | solution.py:22
  (6 other events, 22.8 us)
Sparse Core Ops, SparseCore 0:
  33.7 30.3 reduce-scatter.2
  89.1 29.0 reduce-scatter.4
where the time goes:
time: 128 us; the launch traced here: 127 us
  waiting for transfers between devices  42.6 us (33%)
  blocking collectives  29.1 us (23%)
  local copies, waits for them, and re-layouts  16.6 us (13%)
  between operations  14.6 us (11%)
  matrix products  12.2 us (10%)
  starting transfers between devices  6.54 us (5%)
  other arithmetic  5.5 us (4%)
    reduce_scatter x2, waiting for transfers between devices, per_device(): lax.psum_scatter(partial_terms, 'tm', scatter_dimension=2, tiled=True)  42.6 us
    all_gather x2, blocking collectives, per_device(): zone_coeffs = lax.all_gather(own_field, 'tm', axis=2, tiled=True)  29.1 us
    dot_general x2, matrix products, per_device(): jnp.einsum('th,hdn->tdn', synthesis, zone_coeffs, precision=FULL_PRECISION)  5.57 us
    dot_general x2, matrix products, per_device(): jnp.einsum('th,tdn->hdn', analysis, forces_time, precision=FULL_PRECISION)  4.74 us
    gather x1, local copies, waits for them, and re-layouts, coupled_update(): jnp.diagonal(stiffness[:, 0].astype(jnp.float32), axis1=-2, axis2=-1)  4.56 us
    ppermute x2, starting transfers between devices, padded(): lax.ppermute(head, axis, [((i + 1) % count, i) for i in range(count)])  3.47 us
    gather x1, local copies, waits for them, and re-layouts, coupled_update(): mass_diag = jnp.diagonal(mass_tiles.astype(jnp.float32), axis1=-2, axis2=-1)  3.45 us
    ppermute x2, starting transfers between devices, padded(): lax.ppermute(tail, axis, [(i, (i + 1) % count) for i in range(count)])  2.99 us
  transfers between devices with their start and end apart: 6, of which 2 were waited for; matrix products, arithmetic and copies ran while one was open for 25% of the time, Pallas kernels for 0%

commit v1 on v0

--- a/solution.py
+++ b/solution.py
@@ -135,7 +135,18 @@
     analysis = analysis_table(synthesis, coeff_count, total_samples)
     residual = own_field
     for iteration in range(ITERS):
-        zone_coeffs = lax.all_gather(own_field, "tm", axis=2, tiled=True)
+        peers, place, width_2 = (lax.axis_size("tm"), lax.axis_index("tm"), own_field.shape[2])
+        forward = [(i_2, (i_2 + 1) % peers) for i_2 in range(peers)]
+        whole = jnp.zeros(
+            (*own_field.shape[:2], peers * width_2, *own_field.shape[2 + 1 :]), own_field.dtype
+        )
+        block = own_field
+        for turn in range(peers):
+            holder = (place - turn) % peers
+            whole = lax.dynamic_update_slice_in_dim(whole, block, holder * width_2, axis=2)
+            if turn < peers - 1:
+                block = lax.ppermute(block, "tm", forward)
+        zone_coeffs = whole
         sectors = padded(own_field[:, :, None, :], (("zone", 2),), 1)
         motion = jnp.einsum("th,hdn->tdn", synthesis, zone_coeffs, precision=FULL_PRECISION)
         forces_time = contact_law(

time: 128 us -> 176 us (1.38)
  waiting for transfers between devices: 42.6 us -> 114 us
  blocking collectives: 29.1 us -> 0 us
  other arithmetic: 5.5 us -> 8.6 us
  starting transfers between devices: 6.54 us -> 9.3 us
    ppermute x0 -> x14, waiting for transfers between devices: none -> 59.4 us  [per_device(): block = lax.ppermute(block, 'tm', forward)]
    all_gather x2 -> x0, blocking collectives: 29.1 us -> none  [per_device(): zone_coeffs = lax.all_gather(own_field, 'tm', axis=2, tiled=True)]
    reduce_scatter x2, waiting for transfers between devices: 42.6 us -> 54.1 us  [per_device(): lax.psum_scatter(partial_terms, 'tm', scatter_dimension=2, tiled=True)]
    ppermute x0 -> x14, starting transfers between devices: none -> 2.23 us  [per_device(): block = lax.ppermute(block, 'tm', forward)]
  transfers between devices with their start and end apart: 6 -> 20, of which waited for: 2 -> 16; matrix products, arithmetic and copies ran while one was open for 25% -> 9% of each run, Pallas kernels for 0% -> 0%
where the time goes in v1:
time: 176 us
  waiting for transfers between devices  114 us (65%)
  local copies, waits for them, and re-layouts  15.9 us (9%)
  between operations  15 us (9%)
  matrix products  13.2 us (8%)
  starting transfers between devices  9.3 us (5%)
  other arithmetic  8.6 us (5%)
    ppermute x14, waiting for transfers between devices, per_device(): block = lax.ppermute(block, 'tm', forward)  59.4 us
    reduce_scatter x2, waiting for transfers between devices, per_device(): lax.psum_scatter(partial_terms, 'tm', scatter_dimension=2, tiled=True)  54.1 us
    dot_general x2, matrix products, per_device(): jnp.einsum('th,hdn->tdn', synthesis, zone_coeffs, precision=FULL_PRECISION)  6.56 us
    dot_general x2, matrix products, per_device(): jnp.einsum('th,tdn->hdn', analysis, forces_time, precision=FULL_PRECISION)  4.78 us
    ppermute x2, starting transfers between devices, padded(): lax.ppermute(tail, axis, [(i, (i + 1) % count) for i in range(count)])  4.52 us
  transfers between devices with their start and end apart: 20, of which 16 were waited for; matrix products, arithmetic and copies ran while one was open for 9% of the time, Pallas kernels for 0%

profile of v1, /device:TPU:0, one launch (start us, length us, event | category | flops | bytes accessed | tf_op | source)
XLA Modules:
  0.0 175.8 jit_solution(16998145801616200438)
XLA Ops:
  7.2 3.0 %collective-permute-start = (f32[15,3,1,128]{3,2,1,0:T(1,128)}, f32[15,3,1,128]{3,2,1,0:T(1,128)S(1)}, u32[]{:S(2)}, u32[]{:S(2)}) collective-permute-start(f32[15,3,1,128]{3,2,1,0:T(1,128)} %param.10), channel_id=1, source_target_pairs={{0,1},{1,2},{2,3},{3,0},{4,5},{5,6},{6,7},{7,4},{8,9},{9,10},{10,1... | collective-permute-start | bytes 69128 | tf_op jit(solution)/shard_map/ppermute | solution.py:22
  17.3 3.4 %gather_fusion.1 = f32[384]{0:T(512)S(1)} fusion(f32[384,384]{1,0:T(8,128)S(1)} %fusion.32, s32[384]{0:T(512)S(1)} %or_reduce_fusion), kind=kCustom, calls=%fused_computation.1 | custom fusion | bytes 6144 | tf_op jit(solution)/shard_map/jit(diagonal)/gather | solution.py:101
  20.8 3.4 %gather_fusion.2 = f32[384]{0:T(512)S(1)} fusion(f32[384,384]{1,0:T(8,128)S(1)} %bitcast_convert_fusion, s32[384]{0:T(512)S(1)} %or_reduce_fusion), kind=kCustom, calls=%fused_computation.2 | custom fusion | bytes 6144 | tf_op jit(solution)/shard_map/jit(diagonal)/gather | solution.py:102
  24.3 2.1 %collective-permute-start.3 = (f32[15,3,128]{2,0,1:T(8,128)S(1)}, f32[15,3,128]{2,0,1:T(8,128)S(1)}, u32[]{:S(2)}, u32[]{:S(2)}) collective-permute-start(f32[15,3,128]{2,0,1:T(8,128)S(1)} %collective-permute-done.2), channel_id=1, source_target_pairs={{0,4},{4,8},{8,12},{12,16},{16,20},{20,24},{24,28},{28,0},{1,5},{5... | collective-permute-start | bytes 69128 | tf_op jit(solution)/shard_map/ppermute | solution.py:148
  26.5 2.9 %collective-permute-done.3 = f32[15,3,128]{2,0,1:T(8,128)S(1)} collective-permute-done((f32[15,3,128]{2,0,1:T(8,128)S(1)}, f32[15,3,128]{2,0,1:T(8,128)S(1)}, u32[]{:S(2)}, u32[]{:S(2)}) %collective-permute-start.3) | collective-permute-done | bytes 23072 | tf_op jit(solution)/shard_map/ppermute | solution.py:148
  29.4 5.0 %collective-permute-done.4 = f32[15,3,128]{2,0,1:T(8,128)S(1)} collective-permute-done((f32[15,3,128]{2,0,1:T(8,128)S(1)}, f32[15,3,128]{2,0,1:T(8,128)S(1)}, u32[]{:S(2)}, u32[]{:S(2)}) %collective-permute-start.4) | collective-permute-done | bytes 23072 | tf_op jit(solution)/shard_map/ppermute | solution.py:148
  34.5 5.0 %collective-permute-done.5 = f32[15,3,128]{2,0,1:T(8,128)S(1)} collective-permute-done((f32[15,3,128]{2,0,1:T(8,128)S(1)}, f32[15,3,128]{2,0,1:T(8,128)S(1)}, u32[]{:S(2)}, u32[]{:S(2)}) %collective-permute-start.5) | collective-permute-done | bytes 23072 | tf_op jit(solution)/shard_map/ppermute | solution.py:148
  39.5 5.0 %collective-permute-done.6 = f32[15,3,128]{2,0,1:T(8,128)S(1)} collective-permute-done((f32[15,3,128]{2,0,1:T(8,128)S(1)}, f32[15,3,128]{2,0,1:T(8,128)S(1)}, u32[]{:S(2)}, u32[]{:S(2)}) %collective-permute-start.6) | collective-permute-done | bytes 23072 | tf_op jit(solution)/shard_map/ppermute | solution.py:148
  44.6 5.0 %collective-permute-done.7 = f32[15,3,128]{2,0,1:T(8,128)S(1)} collective-permute-done((f32[15,3,128]{2,0,1:T(8,128)S(1)}, f32[15,3,128]{2,0,1:T(8,128)S(1)}, u32[]{:S(2)}, u32[]{:S(2)}) %collective-permute-start.7) | collective-permute-done | bytes 23072 | tf_op jit(solution)/shard_map/ppermute | solution.py:148
  49.6 5.0 %collective-permute-done.8 = f32[15,3,128]{2,0,1:T(8,128)S(1)} collective-permute-done((f32[15,3,128]{2,0,1:T(8,128)S(1)}, f32[15,3,128]{2,0,1:T(8,128)S(1)}, u32[]{:S(2)}, u32[]{:S(2)}) %collective-permute-start.8) | collective-permute-done | bytes 23072 | tf_op jit(solution)/shard_map/ppermute | solution.py:148
  54.7 2.8 %fusion.54 = f32[256,3,1024]{2,0,1:T(8,128)S(1)} fusion(f32[15,3,1024]{2,0,1:T(8,128)S(1)} %constant_dynamic-update-slice_fusion.8, s32[15]{0:T(128)S(1)} %and_select_fusion.1, s32[256]{0:T(256)S(1)} %iota_add_fusion, pred[15]{0:T(512)(128)(4,1)S(1)} %compare_and_fusion), kind=kOutput, calls=%fused_computation.80 | convolution fusion | flops 141615360 | bytes 3331147 | tf_op jit(solution)/shard_map/th,hdn->tdn/dot_general | solution.py:151
  59.1 2.4 %fusion = f32[15,3,1024]{2,0,1:T(8,128)} fusion(f32[256,1,1024]{2,0,1:T(8,128)S(1)} %fusion.30, f32[256,1,1024]{2,0,1:T(8,128)S(1)} %get-tuple-element.14, f32[256,1,1024]{2,0,1:T(8,128)S(1)} %get-tuple-element.15, f32[15]{0:T(128)S(1)} %fusion.66, s32[15]{0:T(128)S(1)} %and_select_fusion.1, s32[256]{0:T(256)S(1)} %iota_add_fusion, ...), kind=kOutput, calls=%fused_computation.4 | convolution fusion | flops 143192064 | bytes 3331207 | tf_op jit(solution)/shard_map/th,tdn->hdn/dot_general | solution.py:155
  63.2 26.5 %reduce-scatter.3.cloned.1.call-done = f32[15,3,128]{2,0,1:T(8,128)} async-done(((f32[15,3,1024]{2,0,1:T(8,128)}), f32[15,3,128]{2,0,1:T(8,128)}) %reduce-scatter.3.cloned.1.call-update) | async-done | bytes 23056 | tf_op jit(solution)/shard_map/reduce_scatter | solution.py:156
  93.7 2.0 %collective-permute-done.11 = f32[15,3,128]{2,0,1:T(8,128)S(1)} collective-permute-done((f32[15,3,128]{2,0,1:T(8,128)S(1)}, f32[15,3,128]{2,0,1:T(8,128)S(1)}, u32[]{:S(2)}, u32[]{:S(2)}) %collective-permute-start.11) | collective-permute-done | bytes 23072 | tf_op jit(solution)/shard_map/ppermute | solution.py:148
  96.7 4.1 %collective-permute-done.12 = f32[15,3,128]{2,0,1:T(8,128)S(1)} collective-permute-done((f32[15,3,128]{2,0,1:T(8,128)S(1)}, f32[15,3,128]{2,0,1:T(8,128)S(1)}, u32[]{:S(2)}, u32[]{:S(2)}) %collective-permute-start.12) | collective-permute-done | bytes 23072 | tf_op jit(solution)/shard_map/ppermute | solution.py:148
  100.8 5.0 %collective-permute-done.13 = f32[15,3,128]{2,0,1:T(8,128)S(1)} collective-permute-done((f32[15,3,128]{2,0,1:T(8,128)S(1)}, f32[15,3,128]{2,0,1:T(8,128)S(1)}, u32[]{:S(2)}, u32[]{:S(2)}) %collective-permute-start.13) | collective-permute-done | bytes 23072 | tf_op jit(solution)/shard_map/ppermute | solution.py:148
  105.8 5.0 %collective-permute-done.14 = f32[15,3,128]{2,0,1:T(8,128)S(1)} collective-permute-done((f32[15,3,128]{2,0,1:T(8,128)S(1)}, f32[15,3,128]{2,0,1:T(8,128)S(1)}, u32[]{:S(2)}, u32[]{:S(2)}) %collective-permute-start.14) | collective-permute-done | bytes 23072 | tf_op jit(solution)/shard_map/ppermute | solution.py:148
  110.9 5.0 %collective-permute-done.15 = f32[15,3,128]{2,0,1:T(8,128)S(1)} collective-permute-done((f32[15,3,128]{2,0,1:T(8,128)S(1)}, f32[15,3,128]{2,0,1:T(8,128)S(1)}, u32[]{:S(2)}, u32[]{:S(2)}) %collective-permute-start.15) | collective-permute-done | bytes 23072 | tf_op jit(solution)/shard_map/ppermute | solution.py:148
  115.9 5.0 %collective-permute-done.16 = f32[15,3,128]{2,0,1:T(8,128)S(1)} collective-permute-done((f32[15,3,128]{2,0,1:T(8,128)S(1)}, f32[15,3,128]{2,0,1:T(8,128)S(1)}, u32[]{:S(2)}, u32[]{:S(2)}) %collective-permute-start.16) | collective-permute-done | bytes 23072 | tf_op jit(solution)/shard_map/ppermute | solution.py:148
  121.0 5.0 %collective-permute-done.17 = f32[15,3,128]{2,0,1:T(8,128)S(1)} collective-permute-done((f32[15,3,128]{2,0,1:T(8,128)S(1)}, f32[15,3,128]{2,0,1:T(8,128)S(1)}, u32[]{:S(2)}, u32[]{:S(2)}) %collective-permute-start.17) | collective-permute-done | bytes 23072 | tf_op jit(solution)/shard_map/ppermute | solution.py:148
  127.4 3.8 %fusion.52 = f32[256,3,1024]{2,0,1:T(8,128)S(1)} fusion(f32[15,3,1024]{2,0,1:T(8,128)} %copy-done.6, s32[15]{0:T(128)} %copy-done.28, s32[256]{0:T(256)} %copy-done.26, pred[15]{0:T(512)(128)(4,1)} %copy-done.30), kind=kOutput, calls=%fused_computation.78 | convolution fusion | flops 141615360 | bytes 3331147 | tf_op jit(solution)/shard_map/th,hdn->tdn/dot_general | solution.py:151
  133.6 1.6 fusion.29
  135.9 2.4 %fusion.6 = f32[15,3,1024]{2,0,1:T(8,128)} fusion(f32[256,1,1024]{2,0,1:T(8,128)S(1)} %fusion.28, f32[256,1,1024]{2,0,1:T(8,128)S(1)} %get-tuple-element.10, f32[256,1,1024]{2,0,1:T(8,128)S(1)} %get-tuple-element.11, f32[15]{0:T(128)S(1)} %copy-done.33, s32[15]{0:T(128)S(1)} %copy-done.29, s32[256]{0:T(256)S(1)} %copy-done.27, pred[15]{0:T(512)(128)(4,1)S(1)} %copy-done.31), kind=kOutput, calls=%fused_computation.10 | convolution fusion | flops 143192064 | bytes 3331207 | tf_op jit(solution)/shard_map/th,tdn->hdn/dot_general | solution.py:155
  139.3 27.6 %reduce-scatter.5.cloned.1.call-done = f32[15,3,128]{2,0,1:T(8,128)} async-done(((f32[15,3,1024]{2,0,1:T(8,128)}), f32[15,3,128]{2,0,1:T(8,128)}) %reduce-scatter.5.cloned.1.call-update) | async-done | bytes 23056 | tf_op jit(solution)/shard_map/reduce_scatter | solution.py:156
  (156 shorter events, 22.4 us)
Async XLA Ops:
  7.2 82.5 %reduce-scatter.3.cloned.1.call-start = ((), (), s32[]{:S(2)}) async-start(), calls=%async_computation.2 | async-start | bytes 221184 | tf_op jit(solution)/shard_map/reduce_scatter | solution.py:156
  7.2 19.3 %collective-permute-start = (f32[15,3,1,128]{3,2,1,0:T(1,128)}, f32[15,3,1,128]{3,2,1,0:T(1,128)S(1)}, u32[]{:S(2)}, u32[]{:S(2)}) collective-permute-start(f32[15,3,1,128]{3,2,1,0:T(1,128)} %param.10), channel_id=1, source_target_pairs={{0,1},{1,2},{2,3},{3,0},{4,5},{5,6},{6,7},{7,4},{8,9},{9,10},{10,1... | collective-permute-start | bytes 69128 | tf_op jit(solution)/shard_map/ppermute | solution.py:22
  10.2 16.3 %collective-permute-start.1 = (f32[15,3,1,128]{3,2,1,0:T(1,128)}, f32[15,3,1,128]{3,2,1,0:T(1,128)S(1)}, u32[]{:S(2)}, u32[]{:S(2)}) collective-permute-start(f32[15,3,1,128]{3,2,1,0:T(1,128)} %param.10), channel_id=1, source_target_pairs={{1,0},{2,1},{3,2},{0,3},{5,4},{6,5},{7,6},{4,7},{9,8},{10,9},{11,1... | collective-permute-start | bytes 69128 | tf_op jit(solution)/shard_map/ppermute | solution.py:24
  12.0 12.3 %collective-permute-start.2 = (f32[15,3,128]{2,0,1:T(8,128)S(1)}, f32[15,3,128]{2,0,1:T(8,128)S(1)}, u32[]{:S(2)}, u32[]{:S(2)}) collective-permute-start(f32[15,3,128]{2,0,1:T(8,128)S(1)} %bitcast.126), channel_id=1, source_target_pairs={{0,4},{4,8},{8,12},{12,16},{16,20},{20,24},{24,28},{28,0},{1,5},{5... | collective-permute-start | bytes 69128 | tf_op jit(solution)/shard_map/ppermute | solution.py:148
  12.8 48.9 %copy-start.25 = (s32[1024]{0:T(1024)}, s32[1024]{0:T(1024)S(1)}, u32[]{:S(2)}) copy-start(s32[1024]{0:T(1024)S(1)} %pad_clamp_fusion) | copy-start | bytes 12292
  15.6 74.2 %copy-start.23 = (f32[15]{0:T(128)}, f32[15]{0:T(128)S(1)}, u32[]{:S(2)}) copy-start(f32[15]{0:T(128)S(1)} %multiply_multiply_fusion) | copy-start | bytes 184
  20.7 69.0 %copy-start.17 = (f32[384]{0:T(512)}, f32[384]{0:T(512)S(1)}, u32[]{:S(2)}) copy-start(f32[384]{0:T(512)S(1)} %gather_fusion.1) | copy-start | bytes 4612
  24.3 65.5 %copy-start.19 = (f32[384]{0:T(512)}, f32[384]{0:T(512)S(1)}, u32[]{:S(2)}) copy-start(f32[384]{0:T(512)S(1)} %gather_fusion.2) | copy-start | bytes 4612
  24.3 5.1 %collective-permute-start.3 = (f32[15,3,128]{2,0,1:T(8,128)S(1)}, f32[15,3,128]{2,0,1:T(8,128)S(1)}, u32[]{:S(2)}, u32[]{:S(2)}) collective-permute-start(f32[15,3,128]{2,0,1:T(8,128)S(1)} %collective-permute-done.2), channel_id=1, source_target_pairs={{0,4},{4,8},{8,12},{12,16},{16,20},{20,24},{24,28},{28,0},{1,5},{5... | collective-permute-start | bytes 69128 | tf_op jit(solution)/shard_map/ppermute | solution.py:148
  29.4 5.0 %collective-permute-start.4 = (f32[15,3,128]{2,0,1:T(8,128)S(1)}, f32[15,3,128]{2,0,1:T(8,128)S(1)}, u32[]{:S(2)}, u32[]{:S(2)}) collective-permute-start(f32[15,3,128]{2,0,1:T(8,128)S(1)} %collective-permute-done.3), channel_id=1, source_target_pairs={{0,4},{4,8},{8,12},{12,16},{16,20},{20,24},{24,28},{28,0},{1,5},{5... | collective-permute-start | bytes 69128 | tf_op jit(solution)/shard_map/ppermute | solution.py:148
  34.5 5.0 %collective-permute-start.5 = (f32[15,3,128]{2,0,1:T(8,128)S(1)}, f32[15,3,128]{2,0,1:T(8,128)S(1)}, u32[]{:S(2)}, u32[]{:S(2)}) collective-permute-start(f32[15,3,128]{2,0,1:T(8,128)S(1)} %collective-permute-done.4), channel_id=1, source_target_pairs={{0,4},{4,8},{8,12},{12,16},{16,20},{20,24},{24,28},{28,0},{1,5},{5... | collective-permute-start | bytes 69128 | tf_op jit(solution)/shard_map/ppermute | solution.py:148
  39.5 5.0 %collective-permute-start.6 = (f32[15,3,128]{2,0,1:T(8,128)S(1)}, f32[15,3,128]{2,0,1:T(8,128)S(1)}, u32[]{:S(2)}, u32[]{:S(2)}) collective-permute-start(f32[15,3,128]{2,0,1:T(8,128)S(1)} %collective-permute-done.5), channel_id=1, source_target_pairs={{0,4},{4,8},{8,12},{12,16},{16,20},{20,24},{24,28},{28,0},{1,5},{5... | collective-permute-start | bytes 69128 | tf_op jit(solution)/shard_map/ppermute | solution.py:148
  44.6 5.0 %collective-permute-start.7 = (f32[15,3,128]{2,0,1:T(8,128)S(1)}, f32[15,3,128]{2,0,1:T(8,128)S(1)}, u32[]{:S(2)}, u32[]{:S(2)}) collective-permute-start(f32[15,3,128]{2,0,1:T(8,128)S(1)} %collective-permute-done.6), channel_id=1, source_target_pairs={{0,4},{4,8},{8,12},{12,16},{16,20},{20,24},{24,28},{28,0},{1,5},{5... | collective-permute-start | bytes 69128 | tf_op jit(solution)/shard_map/ppermute | solution.py:148
  49.6 5.0 %collective-permute-start.8 = (f32[15,3,128]{2,0,1:T(8,128)S(1)}, f32[15,3,128]{2,0,1:T(8,128)S(1)}, u32[]{:S(2)}, u32[]{:S(2)}) collective-permute-start(f32[15,3,128]{2,0,1:T(8,128)S(1)} %collective-permute-done.7), channel_id=1, source_target_pairs={{0,4},{4,8},{8,12},{12,16},{16,20},{20,24},{24,28},{28,0},{1,5},{5... | collective-permute-start | bytes 69128 | tf_op jit(solution)/shard_map/ppermute | solution.py:148
  61.5 105.3 %reduce-scatter.5.cloned.1.call-start = ((), (), s32[]{:S(2)}) async-start(), calls=%async_computation.3 | async-start | bytes 221184 | tf_op jit(solution)/shard_map/reduce_scatter | solution.py:156
  90.6 5.1 %collective-permute-start.11 = (f32[15,3,128]{2,0,1:T(8,128)S(1)}, f32[15,3,128]{2,0,1:T(8,128)S(1)}, u32[]{:S(2)}, u32[]{:S(2)}) collective-permute-start(f32[15,3,128]{2,0,1:T(8,128)S(1)} %get-tuple-element.13), channel_id=1, source_target_pairs={{0,4},{4,8},{8,12},{12,16},{16,20},{20,24},{24,28},{28,0},{1,5},{5... | collective-permute-start | bytes 69128 | tf_op jit(solution)/shard_map/ppermute | solution.py:148
  90.7 5.0 %collective-permute-start.9 = (f32[15,3,1,128]{3,0,1,2:T(8,128)S(1)}, f32[15,3,1,128]{3,0,1,2:T(8,128)S(1)}, u32[]{:S(2)}, u32[]{:S(2)}) collective-permute-start(f32[15,3,1,128]{3,0,1,2:T(8,128)S(1)} %bitcast.109), channel_id=1, source_target_pairs={{0,1},{1,2},{2,3},{3,0},{4,5},{5,6},{6,7},{7,4},{8,9},{9,10},{10,1... | collective-permute-start | bytes 69128 | tf_op jit(solution)/shard_map/ppermute | solution.py:22
  92.2 3.8 %collective-permute-start.10 = (f32[15,3,1,128]{3,0,1,2:T(8,128)S(1)}, f32[15,3,1,128]{3,0,1,2:T(8,128)S(1)}, u32[]{:S(2)}, u32[]{:S(2)}) collective-permute-start(f32[15,3,1,128]{3,0,1,2:T(8,128)S(1)} %bitcast.110), channel_id=1, source_target_pairs={{1,0},{2,1},{3,2},{0,3},{5,4},{6,5},{7,6},{4,7},{9,8},{10,9},{11,1... | collective-permute-start | bytes 69128 | tf_op jit(solution)/shard_map/ppermute | solution.py:24
  95.7 5.0 %collective-permute-start.12 = (f32[15,3,128]{2,0,1:T(8,128)S(1)}, f32[15,3,128]{2,0,1:T(8,128)S(1)}, u32[]{:S(2)}, u32[]{:S(2)}) collective-permute-start(f32[15,3,128]{2,0,1:T(8,128)S(1)} %collective-permute-done.11), channel_id=1, source_target_pairs={{0,4},{4,8},{8,12},{12,16},{16,20},{20,24},{24,28},{28,0},{1,5},{5... | collective-permute-start | bytes 69128 | tf_op jit(solution)/shard_map/ppermute | solution.py:148
  100.7 5.0 %collective-permute-start.13 = (f32[15,3,128]{2,0,1:T(8,128)S(1)}, f32[15,3,128]{2,0,1:T(8,128)S(1)}, u32[]{:S(2)}, u32[]{:S(2)}) collective-permute-start(f32[15,3,128]{2,0,1:T(8,128)S(1)} %collective-permute-done.12), channel_id=1, source_target_pairs={{0,4},{4,8},{8,12},{12,16},{16,20},{20,24},{24,28},{28,0},{1,5},{5... | collective-permute-start | bytes 69128 | tf_op jit(solution)/shard_map/ppermute | solution.py:148
  105.8 5.0 %collective-permute-start.14 = (f32[15,3,128]{2,0,1:T(8,128)S(1)}, f32[15,3,128]{2,0,1:T(8,128)S(1)}, u32[]{:S(2)}, u32[]{:S(2)}) collective-permute-start(f32[15,3,128]{2,0,1:T(8,128)S(1)} %collective-permute-done.13), channel_id=1, source_target_pairs={{0,4},{4,8},{8,12},{12,16},{16,20},{20,24},{24,28},{28,0},{1,5},{5... | collective-permute-start | bytes 69128 | tf_op jit(solution)/shard_map/ppermute | solution.py:148
  110.8 5.0 %collective-permute-start.15 = (f32[15,3,128]{2,0,1:T(8,128)S(1)}, f32[15,3,128]{2,0,1:T(8,128)S(1)}, u32[]{:S(2)}, u32[]{:S(2)}) collective-permute-start(f32[15,3,128]{2,0,1:T(8,128)S(1)} %collective-permute-done.14), channel_id=1, source_target_pairs={{0,4},{4,8},{8,12},{12,16},{16,20},{20,24},{24,28},{28,0},{1,5},{5... | collective-permute-start | bytes 69128 | tf_op jit(solution)/shard_map/ppermute | solution.py:148
  115.9 5.0 %collective-permute-start.16 = (f32[15,3,128]{2,0,1:T(8,128)S(1)}, f32[15,3,128]{2,0,1:T(8,128)S(1)}, u32[]{:S(2)}, u32[]{:S(2)}) collective-permute-start(f32[15,3,128]{2,0,1:T(8,128)S(1)} %collective-permute-done.15), channel_id=1, source_target_pairs={{0,4},{4,8},{8,12},{12,16},{16,20},{20,24},{24,28},{28,0},{1,5},{5... | collective-permute-start | bytes 69128 | tf_op jit(solution)/shard_map/ppermute | solution.py:148
  120.9 5.1 %collective-permute-start.17 = (f32[15,3,128]{2,0,1:T(8,128)S(1)}, f32[15,3,128]{2,0,1:T(8,128)S(1)}, u32[]{:S(2)}, u32[]{:S(2)}) collective-permute-start(f32[15,3,128]{2,0,1:T(8,128)S(1)} %collective-permute-done.16), channel_id=1, source_target_pairs={{0,4},{4,8},{8,12},{12,16},{16,20},{20,24},{24,28},{28,0},{1,5},{5... | collective-permute-start | bytes 69128 | tf_op jit(solution)/shard_map/ppermute | solution.py:148
  (30 other events, 558.1 us)
Sparse Core Ops, SparseCore 0:
  61.7 27.9 reduce-scatter.2
  138.4 28.4 reduce-scatter.4
